TPU v7x, 256 devices: a whole 4x4x8 slice. The times are simulated.
256 devices in a mesh: pb: 16 (over x_lo, z), ka: 8 (over y, core), ha: 2 (over x_hi).
Axes of the slice: x: 4 (x_hi: 2, x_lo: 2; x = x_hi * 2 + x_lo), y: 4, z: 8, core: 2. Of those that a mesh axis runs over, the one named last changes fastest.
Arguments:
- queries: bfloat16 [16384, 4096], P('pb', 'ha'), may hold values from -512 to 512
- keys: bfloat16 [16, 8, 128, 512], P('pb', 'ka', None, 'ha'), may hold values from -6 to 6
- values: bfloat16 [16, 8, 128, 512], P('pb', 'ka', None, 'ha'), may hold values from -6 to 6
- q_order: int32 [128], P('pb'), may hold values from 0 to 127, as said below
- block_mask: int32 [128, 128], P('pb'), may hold values from 0 to 1, as said below
Outputs:
- attended: bfloat16 [16384, 4096], P(('pb', 'ka'), 'ha')
Inputs may be any that keep to these rules, and one draw needn't show every extreme that they name: `q_order`: slots 2m and 2m+1 hold query blocks i and 127 - i for some i, in either order; every block sits in exactly one slot. block_mask[s, b] is 1 only where b <= q_order[s], and block_mask[s, q_order[s]] is 1. For every m and every r below 8, slots 2m and 2m+1 together list at most 8 key blocks b with b % 8 == r, and exactly 8 for some m and r in every draw.
All inputs are finite; a program needn't handle non-finite values.
Results may differ from a plain program's by a relative error of at most 0.0042.
Values may be sent and summed in bfloat16 or wider, within the bound.
A program may use at most 128 MiB of HBM per device.

v0:
```python
import functools
import math

import jax
import jax.numpy as jnp
from jax import lax
from jax.sharding import Mesh
from jax.sharding import PartitionSpec as P

HEAD_DIM = 128
PB = ("pb_0", "pb_1")
PB_KA = ("pb_0", "pb_1", "ka")


masked_score = -1e30


def in_order(pieces, dim):
    shape = list(pieces.shape[1:])
    shape[dim] *= pieces.shape[0]
    return jnp.moveaxis(pieces, 0, dim).reshape(shape)


def gather_in_order(value, axes, order):
    pieces = value
    for k in order:
        pieces = lax.all_gather(pieces, axes[k])
    done = order[::-1]
    back = [done.index(k) for k in range(len(axes))]
    pieces = pieces.transpose(*back, *range(len(axes), pieces.ndim))
    return pieces.reshape(-1, *value.shape)


def gathered_by_axis(value, axes, order, dim):
    return in_order(gather_in_order(value, axes, order), dim)


def sent_to_all(value, axis):
    size = lax.axis_size(axis)
    return lax.all_to_all(
        jnp.broadcast_to(value[None], (size, *value.shape)), axis, 0, 0, tiled=True
    )


def of_everyone(value, axis):
    everything = sent_to_all(value, axis)
    return jnp.max(everything, axis=0)


def sent_together(arrays, axis, dim, along):
    both = jnp.concatenate(arrays, axis=along)
    out, at, gathered = (lax.psum_scatter(both, axis, scatter_dimension=dim, tiled=True), 0, [])
    for a in arrays:
        gathered.append(lax.slice_in_dim(out, at, at + a.shape[along], axis=along))
        at += a.shape[along]
    return tuple(gathered)


def compact(listed, entry_count):
    running = jnp.cumsum(listed, axis=1)
    span_size = listed.shape[1]
    ranks = jnp.arange(entry_count, dtype=jnp.int32)
    picked = (listed[:, None, :] == 1) & (running[:, None, :] == ranks[None, :, None] + 1)
    places = jnp.arange(span_size, dtype=jnp.int32)
    position = jnp.sum(jnp.where(picked, places[None, None, :], 0), axis=2)
    living = jnp.any(picked, axis=2)
    return (position, living)


def unit_scores(key_pool, query_unit, pool_index, owners, living, global_block, query_blocks):
    head_width = query_unit.shape[-1]
    block_rows = query_unit.shape[1]
    query_rows = jnp.take(query_unit, owners, axis=0)
    key_rows = jnp.take(key_pool, pool_index, axis=0)
    scores = jnp.einsum(
        "eigxd,ejgd->egxij", query_rows, key_rows, preferred_element_type=jnp.float32
    )
    scores = scores * (1.0 / math.sqrt(head_width))
    diagonal = global_block == jnp.take(query_blocks, owners, axis=0)
    causal = jnp.arange(block_rows)[:, None] >= jnp.arange(block_rows)[None, :]
    allowed = living[:, None, None, None, None] & (
        jnp.logical_not(diagonal)[:, None, None, None, None] | causal[None, None, None]
    )
    return (jnp.where(allowed, scores, masked_score), allowed)


def unit_peak(key_pool, unit_args):
    query_unit, pool_index, owners, living, global_block, query_blocks = unit_args
    scores, allowed = unit_scores(
        key_pool, query_unit, pool_index, owners, living, global_block, query_blocks
    )
    row_peak = jnp.max(scores, axis=4)
    belongs = owners[:, None] == jnp.arange(query_unit.shape[0])[None, :]
    return jnp.max(
        jnp.where(belongs[:, :, None, None, None], row_peak[:, None], masked_score), axis=0
    )


def unit_sums(key_pool, value_pool, unit_args):
    query_unit, pool_index, owners, living, global_block, query_blocks, row_tops = unit_args
    scores, allowed = unit_scores(
        key_pool, query_unit, pool_index, owners, living, global_block, query_blocks
    )
    top_rows = jnp.take(row_tops, owners, axis=0)
    weights = jnp.where(allowed, jnp.exp(scores - top_rows[..., None]), 0.0)
    value_rows = jnp.take(value_pool, pool_index, axis=0)
    partial_sum = jnp.einsum(
        "egxij,ejgd->eigxd",
        weights.astype(jnp.bfloat16),
        value_rows,
        preferred_element_type=jnp.float32,
    )
    belongs = (owners[:, None] == jnp.arange(query_unit.shape[0])[None, :]).astype(jnp.float32)
    numerator = jnp.einsum("es,eigxd->sigxd", belongs, partial_sum, precision=lax.Precision.HIGHEST)
    denominator = jnp.einsum("es,egxij->sigx", belongs, weights, precision=lax.Precision.HIGHEST)
    return (numerator, denominator)


def on_device(queries, keys, values, q_order, block_mask):
    head_width = HEAD_DIM
    block_rows = keys.shape[2]
    kv_local = keys.shape[3] // head_width
    q_local = queries.shape[1] // head_width
    group_size = q_local // kv_local
    slot_count = queries.shape[0] // block_rows
    residues = lax.axis_size("ka")
    key_index = lax.axis_index("ka")
    near_keys, near_values = (
        gathered_by_axis(keys, PB, (0, 1), 0),
        gathered_by_axis(values, PB, (0, 1), 0),
    )
    class_blocks = near_keys.shape[0]
    pair_cap = class_blocks // 2
    queried = queries.reshape(slot_count, block_rows, kv_local, group_size, head_width)
    key_pool = near_keys.reshape(class_blocks, block_rows, kv_local, head_width)
    value_pool = near_values.reshape(class_blocks, block_rows, kv_local, head_width)
    listed = block_mask.reshape(slot_count, class_blocks, residues)
    listed = lax.dynamic_index_in_dim(listed, key_index, 2, keepdims=False)
    listed = listed.reshape(slot_count // 2, 2 * class_blocks)
    position, living = compact(listed, pair_cap)
    owners = position // class_blocks
    pool_index = position % class_blocks
    global_block = pool_index * residues + key_index
    query_units = queried.reshape(slot_count // 2, 2, block_rows, kv_local, group_size, head_width)
    query_blocks = q_order.reshape(slot_count // 2, 2)
    unit_args = (query_units, pool_index, owners, living, global_block, query_blocks)
    row_tops = lax.map(functools.partial(unit_peak, key_pool), unit_args)
    row_tops = of_everyone(row_tops, "ka")
    numerator, denominator = lax.map(
        functools.partial(unit_sums, key_pool, value_pool), unit_args + (row_tops,)
    )
    numerator = numerator.reshape(slot_count * block_rows, q_local * head_width)
    denominator = denominator.reshape(slot_count * block_rows, q_local)
    numerator, denominator = sent_together((numerator, denominator), "ka", 0, 1)
    attended = numerator.reshape(-1, q_local, head_width) / denominator[:, :, None]
    return attended.astype(jnp.bfloat16).reshape(-1, q_local * head_width)


def solution(mesh):
    split = Mesh(
        mesh.devices.reshape(2, 8, mesh.shape["ka"], mesh.shape["ha"]), ("pb_0", "pb_1", "ka", "ha")
    )
    in_specs = (P(PB, "ha"), P(PB, "ka", None, "ha"), P(PB, "ka", None, "ha"), P(PB), P(PB, None))
    out_specs = P(PB_KA, "ha")
    return jax.shard_map(
        on_device, mesh=split, in_specs=in_specs, out_specs=out_specs, check_vma=False
    )
```

profile of v0, /device:TPU:1, one launch (start us, length us, event | category | flops | bytes accessed | tf_op | source)
XLA Modules:
  0.0 389.6 jit_solution(9207610490852502496)
XLA Ops:
  6.5 6.2 %all-gather.2 = bf16[2,1,128,256]{3,2,1,0:T(8,128)(2,1)} all-gather(bf16[1,1,128,256]{3,2,1,0:T(8,128)(2,1)} %param.16), channel_id=4, replica_groups=mesh['pb_0'=2,'pb_1'=8,'ka'=8,'ha'=2] {'pb_0'}, dimensions={0}, use_global_device_ids=true | all-gather | bytes 196608 | tf_op jit(solution)/shard_map/all_gather | solution.py:27
  12.8 4.1 %all-gather = bf16[2,1,128,256]{3,2,1,0:T(8,128)(2,1)} all-gather(bf16[1,1,128,256]{3,2,1,0:T(8,128)(2,1)} %param.17), channel_id=2, replica_groups=mesh['pb_0'=2,'pb_1'=8,'ka'=8,'ha'=2] {'pb_0'}, dimensions={0}, use_global_device_ids=true | all-gather | bytes 196608 | tf_op jit(solution)/shard_map/all_gather | solution.py:27
  18.8 5.6 %copy.76 = bf16[128,8,16,128]{3,2,1,0:T(8,128)(2,1)} copy(bf16[128,8,16,128]{3,1,2,0:T(8,128)(2,1)} %bitcast.165) | data formatting | bytes 8388608
  24.5 25.4 %all-gather.9.cloned.1.call-done = bf16[16,1,128,256]{3,2,1,0:T(8,128)(2,1)} async-done(((bf16[2,1,128,256]{3,2,1,0:T(8,128)(2,1)}), bf16[16,1,128,256]{3,2,1,0:T(8,128)(2,1)}) %all-gather.9.cloned.1.call-update) | async-done | bytes 1048592 | tf_op jit(solution)/shard_map/all_gather | solution.py:27
  51.5 66.7 %while.22 = (s32[]{:T(128)}, f32[4,2,2,8,128]{4,3,2,1,0:T(8,128)S(1)}, s32[4,8]{1,0:T(4,128)S(1)}, pred[4,8]{1,0:T(4,128)(4,1)S(1)}, s32[4,8]{1,0:T(4,128)S(1)},...) while((s32[]{:T(128)}, ...), condition=%wide.region_6.10_spmd, body=%wide.region_3.9_spmd.sunk | while | flops 545847488 | bytes 26174228 | solution.py:147
  53.8 3.0 gather_fusion.1
  56.8 4.6 %broadcast_select_fusion.9 = bf16[8,128,2,8,128]{4,3,2,1,0:T(8,128)(2,1)} fusion(bf16[8,128,2,8,128]{4,3,2,1,0:T(8,128)(2,1)} %gather_fusion.1, pred[8]{0:T(512)(128)(4,1)S(1)} %get-tuple-element.311), kind=kLoop, calls=%fused_computation.12.clone.1 | loop fusion | flops 2097152 | bytes 8388616 | tf_op jit(solution)/shard_map/while/body/eval_jaxpr/jit(_take)/select_n | solution.py:73
  61.4 1.6 gather_fusion.2
  63.5 4.4 %fusion.75 = f32[8,2,8,128]{3,2,1,0:T(8,128)S(1)} fusion(pred[8,128,128]{1,2,0:T(8,128)(4,1)S(1)} %or_and_fusion.4, bf16[8,128,2,8,128]{4,3,2,1,0:T(8,128)(2,1)} %broadcast_select_fusion.9, bf16[8,128,2,128,1]{3,2,1,0,4:T(2,128)(2,1)S(1)} %fusion.74), kind=kOutput, calls=%fused_computation.9.clone.1 | convolution fusion | flops 543145984 | bytes 4915200 | tf_op jit(solution)/shard_map/while/body/eval_jaxpr/eigxd,ejgd->egxij/dot_general | solution.py:75
  70.5 3.0 gather_fusion.1
  73.5 4.6 %broadcast_select_fusion.9 = bf16[8,128,2,8,128]{4,3,2,1,0:T(8,128)(2,1)} fusion(bf16[8,128,2,8,128]{4,3,2,1,0:T(8,128)(2,1)} %gather_fusion.1, pred[8]{0:T(512)(128)(4,1)S(1)} %get-tuple-element.311), kind=kLoop, calls=%fused_computation.12.clone.1 | loop fusion | flops 2097152 | bytes 8388616 | tf_op jit(solution)/shard_map/while/body/eval_jaxpr/jit(_take)/select_n | solution.py:73
  78.1 1.6 gather_fusion.2
  80.2 4.4 %fusion.75 = f32[8,2,8,128]{3,2,1,0:T(8,128)S(1)} fusion(pred[8,128,128]{1,2,0:T(8,128)(4,1)S(1)} %or_and_fusion.4, bf16[8,128,2,8,128]{4,3,2,1,0:T(8,128)(2,1)} %broadcast_select_fusion.9, bf16[8,128,2,128,1]{3,2,1,0,4:T(2,128)(2,1)S(1)} %fusion.74), kind=kOutput, calls=%fused_computation.9.clone.1 | convolution fusion | flops 543145984 | bytes 4915200 | tf_op jit(solution)/shard_map/while/body/eval_jaxpr/eigxd,ejgd->egxij/dot_general | solution.py:75
  87.2 3.0 gather_fusion.1
  90.2 4.6 %broadcast_select_fusion.9 = bf16[8,128,2,8,128]{4,3,2,1,0:T(8,128)(2,1)} fusion(bf16[8,128,2,8,128]{4,3,2,1,0:T(8,128)(2,1)} %gather_fusion.1, pred[8]{0:T(512)(128)(4,1)S(1)} %get-tuple-element.311), kind=kLoop, calls=%fused_computation.12.clone.1 | loop fusion | flops 2097152 | bytes 8388616 | tf_op jit(solution)/shard_map/while/body/eval_jaxpr/jit(_take)/select_n | solution.py:73
  94.7 1.6 gather_fusion.2
  96.9 4.4 %fusion.75 = f32[8,2,8,128]{3,2,1,0:T(8,128)S(1)} fusion(pred[8,128,128]{1,2,0:T(8,128)(4,1)S(1)} %or_and_fusion.4, bf16[8,128,2,8,128]{4,3,2,1,0:T(8,128)(2,1)} %broadcast_select_fusion.9, bf16[8,128,2,128,1]{3,2,1,0,4:T(2,128)(2,1)S(1)} %fusion.74), kind=kOutput, calls=%fused_computation.9.clone.1 | convolution fusion | flops 543145984 | bytes 4915200 | tf_op jit(solution)/shard_map/while/body/eval_jaxpr/eigxd,ejgd->egxij/dot_general | solution.py:75
  103.8 3.0 gather_fusion.1
  106.8 4.6 %broadcast_select_fusion.9 = bf16[8,128,2,8,128]{4,3,2,1,0:T(8,128)(2,1)} fusion(bf16[8,128,2,8,128]{4,3,2,1,0:T(8,128)(2,1)} %gather_fusion.1, pred[8]{0:T(512)(128)(4,1)S(1)} %get-tuple-element.311), kind=kLoop, calls=%fused_computation.12.clone.1 | loop fusion | flops 2097152 | bytes 8388616 | tf_op jit(solution)/shard_map/while/body/eval_jaxpr/jit(_take)/select_n | solution.py:73
  111.4 1.6 gather_fusion.2
  113.5 4.4 %fusion.75 = f32[8,2,8,128]{3,2,1,0:T(8,128)S(1)} fusion(pred[8,128,128]{1,2,0:T(8,128)(4,1)S(1)} %or_and_fusion.4, bf16[8,128,2,8,128]{4,3,2,1,0:T(8,128)(2,1)} %broadcast_select_fusion.9, bf16[8,128,2,128,1]{3,2,1,0,4:T(2,128)(2,1)S(1)} %fusion.74), kind=kOutput, calls=%fused_computation.9.clone.1 | convolution fusion | flops 543145984 | bytes 4915200 | tf_op jit(solution)/shard_map/while/body/eval_jaxpr/eigxd,ejgd->egxij/dot_general | solution.py:75
  119.0 10.0 %all-to-all-start = ((f32[8,4,2,2,8,128]{5,4,3,2,1,0:T(8,128)}), f32[8,4,2,2,8,128]{5,4,3,2,1,0:T(8,128)S(1)}, u32[]{:S(2)}, u32[]{:S(2)}) async-start(f32[8,4,2,2,8,128]{5,4,3,2,1,0:T(8,128)} %broadcast_in_dim.142), calls=%async_computation | async-start | bytes 1048576 | tf_op jit(solution)/shard_map/all_to_all | solution.py:40
  129.0 2.3 copy.55
  132.6 5.7 %all-to-all-done = f32[8,4,2,2,8,128]{5,4,3,2,1,0:T(8,128)S(1)} async-done(((f32[8,4,2,2,8,128]{5,4,3,2,1,0:T(8,128)}), f32[8,4,2,2,8,128]{5,4,3,2,1,0:T(8,128)S(1)}, u32[]{:S(2)}, u32[]{:S(2)}) %all-to-all-start) | async-done | bytes 524320 | tf_op jit(solution)/shard_map/all_to_all | solution.py:40
  138.4 170.0 %while.23 = (s32[]{:T(128)}, f32[4,2,128,2,8,128]{5,4,3,2,1,0:T(8,128)}, f32[4,2,128,2,8]{2,1,0,4,3:T(2,128)S(1)}, s32[4,8]{1,0:T(4,128)S(1)}, s32[4,8]{1,0:T(4,...) while((s32[]{:T(128)}, ...), condition=%wide.region_10.14_spmd, body=%wide.region_8.13_spmd.sunk | while | flops 1148341504 | bytes 94337016 | solution.py:149
  139.5 1.6 gather_fusion.6
  141.1 1.6 gather_fusion.7
  145.1 3.1 gather_fusion.5
  148.2 4.6 %broadcast_select_fusion.11 = bf16[8,128,2,8,128]{4,3,2,1,0:T(8,128)(2,1)} fusion(bf16[8,128,2,8,128]{4,3,2,1,0:T(8,128)(2,1)} %gather_fusion.5, pred[8]{0:T(512)(128)(4,1)S(1)} %get-tuple-element.326), kind=kLoop, calls=%fused_computation.51.clone.1 | loop fusion | flops 2097152 | bytes 8388616 | tf_op jit(solution)/shard_map/while/body/eval_jaxpr/jit(_take)/select_n | solution.py:73
  153.5 5.1 %fusion.86 = (f32[8,2,8,128]{3,2,1,0:T(8,128)S(1)}, f32[8,2,128,128,8]{3,2,4,1,0:T(8,128)S(1)}) fusion(f32[8,2,8,128]{3,2,1,0:T(8,128)S(1)} %broadcast_select_fusion.10, pred[8,128,128]{1,2,0:T(8,128)(4,1)S(1)} %or_and_fusion.5, bf16[8,128,2,8,128]{4,3,2,1,0:T(8,128)(2,1)} %broadcast_select_fusion.11, ...), kind=kOutput, calls=%fused_computation.42.clone.1 | convolution fusion | flops 547340288 | bytes 13369344 | tf_op jit(solution)/shard_map/while/body/eval_jaxpr/eigxd,ejgd->egxij/dot_general | solution.py:75
  158.6 4.5 %fusion.87 = f32[8,128,2,8,128]{1,4,3,2,0:T(8,128)} fusion(f32[8,2,128,128,8]{3,2,4,1,0:T(8,128)S(1)} %get-tuple-element.331, f32[8,2,8,128]{3,2,1,0:T(8,128)S(1)} %broadcast_select_fusion.10, pred[8,128,128]{1,2,0:T(8,128)(4,1)S(1)} %or_and_fusion.5, bf16[8,128,2,128,1]{3,2,1,0,4:T(2,128)(2,1)S(1)} %get-tuple-element.332), kind=kOutput, calls=%fused_computation.53.clone.1 | convolution fusion | flops 547356672 | bytes 17498112 | tf_op jit(solution)/shard_map/while/body/eval_jaxpr/egxij,ejgd->eigxd/dot_general | solution.py:107
  163.0 8.8 %copy.113 = f32[8,128,2,8,128]{4,0,3,2,1:T(8,128)} copy(f32[8,128,2,8,128]{1,4,3,2,0:T(8,128)} %fusion.87) | data formatting | bytes 16777216 | tf_op jit(solution)/shard_map/while/body/eval_jaxpr/egxij,ejgd->eigxd/transpose | solution.py:107
  171.8 7.5 %convolution_bitcast_fusion.3 = f32[1,2,128,2,8,128]{5,1,4,3,2,0:T(2,128)S(1)} fusion(f32[8,128,2,8,128]{4,0,3,2,1:T(8,128)} %copy.113, s32[8]{0:T(128)S(1)} %get-tuple-element.327), kind=kOutput, calls=%fused_computation.55.clone.1 | convolution fusion | flops 50331664 | bytes 10485792 | tf_op jit(solution)/shard_map/while/body/eval_jaxpr/es,eigxd->sigxd/dot_general | solution.py:114
  179.3 1.5 copy_dynamic-update-slice_fusion.2
  182.0 1.6 gather_fusion.6
  183.6 1.6 gather_fusion.7
  187.6 3.1 gather_fusion.5
  190.7 4.6 %broadcast_select_fusion.11 = bf16[8,128,2,8,128]{4,3,2,1,0:T(8,128)(2,1)} fusion(bf16[8,128,2,8,128]{4,3,2,1,0:T(8,128)(2,1)} %gather_fusion.5, pred[8]{0:T(512)(128)(4,1)S(1)} %get-tuple-element.326), kind=kLoop, calls=%fused_computation.51.clone.1 | loop fusion | flops 2097152 | bytes 8388616 | tf_op jit(solution)/shard_map/while/body/eval_jaxpr/jit(_take)/select_n | solution.py:73
  195.9 5.1 %fusion.86 = (f32[8,2,8,128]{3,2,1,0:T(8,128)S(1)}, f32[8,2,128,128,8]{3,2,4,1,0:T(8,128)S(1)}) fusion(f32[8,2,8,128]{3,2,1,0:T(8,128)S(1)} %broadcast_select_fusion.10, pred[8,128,128]{1,2,0:T(8,128)(4,1)S(1)} %or_and_fusion.5, bf16[8,128,2,8,128]{4,3,2,1,0:T(8,128)(2,1)} %broadcast_select_fusion.11, ...), kind=kOutput, calls=%fused_computation.42.clone.1 | convolution fusion | flops 547340288 | bytes 13369344 | tf_op jit(solution)/shard_map/while/body/eval_jaxpr/eigxd,ejgd->egxij/dot_general | solution.py:75
  201.0 4.5 %fusion.87 = f32[8,128,2,8,128]{1,4,3,2,0:T(8,128)} fusion(f32[8,2,128,128,8]{3,2,4,1,0:T(8,128)S(1)} %get-tuple-element.331, f32[8,2,8,128]{3,2,1,0:T(8,128)S(1)} %broadcast_select_fusion.10, pred[8,128,128]{1,2,0:T(8,128)(4,1)S(1)} %or_and_fusion.5, bf16[8,128,2,128,1]{3,2,1,0,4:T(2,128)(2,1)S(1)} %get-tuple-element.332), kind=kOutput, calls=%fused_computation.53.clone.1 | convolution fusion | flops 547356672 | bytes 17498112 | tf_op jit(solution)/shard_map/while/body/eval_jaxpr/egxij,ejgd->eigxd/dot_general | solution.py:107
  205.5 8.8 %copy.113 = f32[8,128,2,8,128]{4,0,3,2,1:T(8,128)} copy(f32[8,128,2,8,128]{1,4,3,2,0:T(8,128)} %fusion.87) | data formatting | bytes 16777216 | tf_op jit(solution)/shard_map/while/body/eval_jaxpr/egxij,ejgd->eigxd/transpose | solution.py:107
  214.3 7.5 %convolution_bitcast_fusion.3 = f32[1,2,128,2,8,128]{5,1,4,3,2,0:T(2,128)S(1)} fusion(f32[8,128,2,8,128]{4,0,3,2,1:T(8,128)} %copy.113, s32[8]{0:T(128)S(1)} %get-tuple-element.327), kind=kOutput, calls=%fused_computation.55.clone.1 | convolution fusion | flops 50331664 | bytes 10485792 | tf_op jit(solution)/shard_map/while/body/eval_jaxpr/es,eigxd->sigxd/dot_general | solution.py:114
  224.4 1.6 gather_fusion.6
  226.0 1.6 gather_fusion.7
  230.0 3.1 gather_fusion.5
  233.1 4.6 %broadcast_select_fusion.11 = bf16[8,128,2,8,128]{4,3,2,1,0:T(8,128)(2,1)} fusion(bf16[8,128,2,8,128]{4,3,2,1,0:T(8,128)(2,1)} %gather_fusion.5, pred[8]{0:T(512)(128)(4,1)S(1)} %get-tuple-element.326), kind=kLoop, calls=%fused_computation.51.clone.1 | loop fusion | flops 2097152 | bytes 8388616 | tf_op jit(solution)/shard_map/while/body/eval_jaxpr/jit(_take)/select_n | solution.py:73
  238.4 5.1 %fusion.86 = (f32[8,2,8,128]{3,2,1,0:T(8,128)S(1)}, f32[8,2,128,128,8]{3,2,4,1,0:T(8,128)S(1)}) fusion(f32[8,2,8,128]{3,2,1,0:T(8,128)S(1)} %broadcast_select_fusion.10, pred[8,128,128]{1,2,0:T(8,128)(4,1)S(1)} %or_and_fusion.5, bf16[8,128,2,8,128]{4,3,2,1,0:T(8,128)(2,1)} %broadcast_select_fusion.11, ...), kind=kOutput, calls=%fused_computation.42.clone.1 | convolution fusion | flops 547340288 | bytes 13369344 | tf_op jit(solution)/shard_map/while/body/eval_jaxpr/eigxd,ejgd->egxij/dot_general | solution.py:75
  243.4 4.5 %fusion.87 = f32[8,128,2,8,128]{1,4,3,2,0:T(8,128)} fusion(f32[8,2,128,128,8]{3,2,4,1,0:T(8,128)S(1)} %get-tuple-element.331, f32[8,2,8,128]{3,2,1,0:T(8,128)S(1)} %broadcast_select_fusion.10, pred[8,128,128]{1,2,0:T(8,128)(4,1)S(1)} %or_and_fusion.5, bf16[8,128,2,128,1]{3,2,1,0,4:T(2,128)(2,1)S(1)} %get-tuple-element.332), kind=kOutput, calls=%fused_computation.53.clone.1 | convolution fusion | flops 547356672 | bytes 17498112 | tf_op jit(solution)/shard_map/while/body/eval_jaxpr/egxij,ejgd->eigxd/dot_general | solution.py:107
  247.9 8.8 %copy.113 = f32[8,128,2,8,128]{4,0,3,2,1:T(8,128)} copy(f32[8,128,2,8,128]{1,4,3,2,0:T(8,128)} %fusion.87) | data formatting | bytes 16777216 | tf_op jit(solution)/shard_map/while/body/eval_jaxpr/egxij,ejgd->eigxd/transpose | solution.py:107
  256.7 7.5 %convolution_bitcast_fusion.3 = f32[1,2,128,2,8,128]{5,1,4,3,2,0:T(2,128)S(1)} fusion(f32[8,128,2,8,128]{4,0,3,2,1:T(8,128)} %copy.113, s32[8]{0:T(128)S(1)} %get-tuple-element.327), kind=kOutput, calls=%fused_computation.55.clone.1 | convolution fusion | flops 50331664 | bytes 10485792 | tf_op jit(solution)/shard_map/while/body/eval_jaxpr/es,eigxd->sigxd/dot_general | solution.py:114
  264.2 1.5 copy_dynamic-update-slice_fusion.2
  266.8 1.6 gather_fusion.6
  268.4 1.6 gather_fusion.7
  272.4 3.1 gather_fusion.5
  275.5 4.6 %broadcast_select_fusion.11 = bf16[8,128,2,8,128]{4,3,2,1,0:T(8,128)(2,1)} fusion(bf16[8,128,2,8,128]{4,3,2,1,0:T(8,128)(2,1)} %gather_fusion.5, pred[8]{0:T(512)(128)(4,1)S(1)} %get-tuple-element.326), kind=kLoop, calls=%fused_computation.51.clone.1 | loop fusion | flops 2097152 | bytes 8388616 | tf_op jit(solution)/shard_map/while/body/eval_jaxpr/jit(_take)/select_n | solution.py:73
  280.8 5.1 %fusion.86 = (f32[8,2,8,128]{3,2,1,0:T(8,128)S(1)}, f32[8,2,128,128,8]{3,2,4,1,0:T(8,128)S(1)}) fusion(f32[8,2,8,128]{3,2,1,0:T(8,128)S(1)} %broadcast_select_fusion.10, pred[8,128,128]{1,2,0:T(8,128)(4,1)S(1)} %or_and_fusion.5, bf16[8,128,2,8,128]{4,3,2,1,0:T(8,128)(2,1)} %broadcast_select_fusion.11, ...), kind=kOutput, calls=%fused_computation.42.clone.1 | convolution fusion | flops 547340288 | bytes 13369344 | tf_op jit(solution)/shard_map/while/body/eval_jaxpr/eigxd,ejgd->egxij/dot_general | solution.py:75
  285.9 4.5 %fusion.87 = f32[8,128,2,8,128]{1,4,3,2,0:T(8,128)} fusion(f32[8,2,128,128,8]{3,2,4,1,0:T(8,128)S(1)} %get-tuple-element.331, f32[8,2,8,128]{3,2,1,0:T(8,128)S(1)} %broadcast_select_fusion.10, pred[8,128,128]{1,2,0:T(8,128)(4,1)S(1)} %or_and_fusion.5, bf16[8,128,2,128,1]{3,2,1,0,4:T(2,128)(2,1)S(1)} %get-tuple-element.332), kind=kOutput, calls=%fused_computation.53.clone.1 | convolution fusion | flops 547356672 | bytes 17498112 | tf_op jit(solution)/shard_map/while/body/eval_jaxpr/egxij,ejgd->eigxd/dot_general | solution.py:107
  290.3 8.8 %copy.113 = f32[8,128,2,8,128]{4,0,3,2,1:T(8,128)} copy(f32[8,128,2,8,128]{1,4,3,2,0:T(8,128)} %fusion.87) | data formatting | bytes 16777216 | tf_op jit(solution)/shard_map/while/body/eval_jaxpr/egxij,ejgd->eigxd/transpose | solution.py:107
  299.1 7.5 %convolution_bitcast_fusion.3 = f32[1,2,128,2,8,128]{5,1,4,3,2,0:T(2,128)S(1)} fusion(f32[8,128,2,8,128]{4,0,3,2,1:T(8,128)} %copy.113, s32[8]{0:T(128)S(1)} %get-tuple-element.327), kind=kOutput, calls=%fused_computation.55.clone.1 | convolution fusion | flops 50331664 | bytes 10485792 | tf_op jit(solution)/shard_map/while/body/eval_jaxpr/es,eigxd->sigxd/dot_general | solution.py:114
  306.6 1.5 copy_dynamic-update-slice_fusion.2
  308.3 9.3 %reshape.168 = f32[1024,2048]{1,0:T(8,128)} reshape(f32[4,2,128,2,8,128]{5,4,3,2,1,0:T(8,128)} %get-tuple-element.119) | data formatting | bytes 16777216 | tf_op jit(solution)/shard_map/reshape | solution.py:152
  317.8 7.6 %pad_maximum_fusion = f32[1024,2064]{1,0:T(8,128)} fusion(f32[1024,16]{1,0:T(8,128)S(1)} %copy.59, f32[1024,2048]{1,0:T(8,128)} %reshape.168), kind=kLoop, calls=%fused_computation.98 | loop fusion | flops 2113536 | bytes 16908288 | tf_op jit(solution)/shard_map/concatenate | solution.py:51
  325.4 54.0 %reduce-scatter.2.cloned.1.call-done = f32[128,2064]{1,0:T(8,128)} async-done(((f32[1024,2064]{1,0:T(8,128)}), f32[128,2064]{1,0:T(8,128)}) %reduce-scatter.2.cloned.1.call-update) | async-done | bytes 1056784 | tf_op jit(solution)/shard_map/reduce_scatter | solution.py:52
  380.6 2.4 fusion.47
  (180 shorter events, 37.0 us)
Async XLA Ops:
  6.5 17.8 %copy-start.2 = (s32[8]{0:T(128)S(1)}, s32[8]{0:T(128)}, u32[]{:S(2)}) copy-start(s32[8]{0:T(128)} %param.18) | copy-start | bytes 100
  6.5 43.3 %all-gather.9.cloned.1.call-start = ((), (), s32[]{:S(2)}) async-start(), calls=%async_computation.4 | async-start | bytes 1179648 | tf_op jit(solution)/shard_map/all_gather | solution.py:27
  12.8 116.2 %all-gather.7.cloned.1.call-start = ((), (), s32[]{:S(2)}) async-start(), calls=%async_computation.3 | async-start | bytes 1179648 | tf_op jit(solution)/shard_map/all_gather | solution.py:27
  119.0 19.3 %all-to-all-start = ((f32[8,4,2,2,8,128]{5,4,3,2,1,0:T(8,128)}), f32[8,4,2,2,8,128]{5,4,3,2,1,0:T(8,128)S(1)}, u32[]{:S(2)}, u32[]{:S(2)}) async-start(f32[8,4,2,2,8,128]{5,4,3,2,1,0:T(8,128)} %broadcast_in_dim.142), calls=%async_computation | async-start | bytes 1048576 | tf_op jit(solution)/shard_map/all_to_all | solution.py:40
  129.0 250.5 %reduce-scatter.2.cloned.1.call-start = ((), (), s32[]{:S(2)}) async-start(), calls=%async_computation.2 | async-start | bytes 10027008 | tf_op jit(solution)/shard_map/reduce_scatter | solution.py:52
  138.6 2.6 copy-start
  171.8 9.2 %copy-start.1 = (bf16[16,128,2,128]{3,2,1,0:T(2,128)(2,1)S(1)}, bf16[16,128,2,128]{3,2,1,0:T(2,128)(2,1)}, u32[]{:S(2)}) copy-start(bf16[16,128,2,128]{3,2,1,0:T(2,128)(2,1)} %copy-done) | copy-start | bytes 3145732 | tf_op jit(solution)/shard_map/while
  181.0 2.6 copy-start
  214.2 9.2 %copy-start.1 = (bf16[16,128,2,128]{3,2,1,0:T(2,128)(2,1)S(1)}, bf16[16,128,2,128]{3,2,1,0:T(2,128)(2,1)}, u32[]{:S(2)}) copy-start(bf16[16,128,2,128]{3,2,1,0:T(2,128)(2,1)} %copy-done) | copy-start | bytes 3145732 | tf_op jit(solution)/shard_map/while
  223.4 2.6 copy-start
  256.7 9.2 %copy-start.1 = (bf16[16,128,2,128]{3,2,1,0:T(2,128)(2,1)S(1)}, bf16[16,128,2,128]{3,2,1,0:T(2,128)(2,1)}, u32[]{:S(2)}) copy-start(bf16[16,128,2,128]{3,2,1,0:T(2,128)(2,1)} %copy-done) | copy-start | bytes 3145732 | tf_op jit(solution)/shard_map/while
  265.9 2.6 copy-start
  299.1 9.2 %copy-start.1 = (bf16[16,128,2,128]{3,2,1,0:T(2,128)(2,1)S(1)}, bf16[16,128,2,128]{3,2,1,0:T(2,128)(2,1)}, u32[]{:S(2)}) copy-start(bf16[16,128,2,128]{3,2,1,0:T(2,128)(2,1)} %copy-done) | copy-start | bytes 3145732 | tf_op jit(solution)/shard_map/while
Sparse Core Ops, SparseCore 0:
  12.9 36.9 all-gather.8
  51.7 36.7 all-gather.6
  325.5 53.8 reduce-scatter.1
where the time goes:
time: 392 us; the launch traced here: 390 us
  local copies, waits for them, and re-layouts  127 us (32%)
  matrix products  86.3 us (22%)
  waiting for transfers between devices  85.2 us (22%)
  other arithmetic  56.2 us (14%)
  between operations  13.2 us (3%)
  blocking collectives  10.3 us (3%)
  starting transfers between devices  10 us (3%)
    reduce_scatter x1, waiting for transfers between devices, sent_together(): lax.psum_scatter(both, axis, scatter_dimension=dim, tiled=True)  54 us
    dot_general x8, matrix products, unit_scores(): jnp.einsum('eigxd,ejgd->egxij', query_rows, key_rows, preferred_element_t...  37.8 us
    select_n x8, other arithmetic, unit_scores(): query_rows = jnp.take(query_unit, owners, axis=0)  36.8 us
    transpose x4, local copies, waits for them, and re-layouts, unit_sums(): jnp.einsum('egxij,ejgd->eigxd', weights.astype(jnp.bfloat16), value_rows,...  35.1 us
    dot_general x4, matrix products, unit_sums(): jnp.einsum('es,eigxd->sigxd', belongs, partial_sum, precision=lax.Precisi...  30 us
    all_gather x2, waiting for transfers between devices, gather_in_order(): pieces = lax.all_gather(pieces, axes[k])  25.4 us
    gather x8, local copies, waits for them, and re-layouts, unit_scores(): query_rows = jnp.take(query_unit, owners, axis=0)  24.3 us
    dot_general x4, matrix products, unit_sums(): jnp.einsum('egxij,ejgd->eigxd', weights.astype(jnp.bfloat16), value_rows,...  17.8 us
  transfers between devices with their start and end apart: 4, of which 3 were waited for; matrix products, arithmetic and copies ran while one was open for 20% of the time, Pallas kernels for 0%

commit v1 on v0

v1 whole, which is shorter than its diff:
```python
import functools
import math

import jax
import jax.numpy as jnp
from jax import lax
from jax.experimental import pallas as pl
from jax.experimental.pallas import tpu as pltpu
from jax.sharding import PartitionSpec as P

MESH = pl.DeviceIdType.MESH
BF16, F32, I32 = jnp.bfloat16, jnp.float32, jnp.int32
D = 128
GROUP = 8
LANES = GROUP * D
RING = 8
POOL = 64
NG = 17
SCALE = math.log2(math.e) / math.sqrt(D)
LOW = -1e30
VMEM_LIMIT = 60 * 1024 * 1024


def head_of(y):
    return lax.rem(lax.div(y + 1, 2), 2)


def gather_kernel(k_ref, v_ref, kbuf, vbuf, send, recv, local):
    pb, ka = lax.axis_index("pb"), lax.axis_index("ka")
    x, z = lax.div(pb, RING), lax.rem(pb, RING)
    y, c = lax.div(ka, 2), lax.rem(ka, 2)
    u = lax.rem(y, 2)
    mate = {"ka": (y + 1 - 2 * u) * 2 + c}
    across = {"pb": (1 - x) * RING + z}
    up = {"pb": x * RING + lax.rem(z + 1, RING)}
    down = {"pb": x * RING + lax.rem(z + RING - 1, RING)}
    sibling = {"ka": y * 2 + 1 - c}
    head = head_of(y)

    barrier = pltpu.get_barrier_semaphore()
    for who in (mate, across, up, down, sibling):
        pl.semaphore_signal(barrier, inc=1, device_id=who, device_id_type=MESH)
    pl.semaphore_wait(barrier, 5)

    started = []
    number = [0]

    def next_id():
        number[0] += 1
        return number[0] - 1

    def move(src, dst, landed, who):
        n = next_id()
        copy = pltpu.make_async_remote_copy(
            src_ref=src, dst_ref=dst, send_sem=send.at[n], recv_sem=recv.at[n],
            device_id=who, device_id_type=MESH,
        )
        copy.start()
        started.append(copy)
        return pltpu.make_async_remote_copy(
            src_ref=src, dst_ref=landed, send_sem=send.at[n], recv_sem=recv.at[n],
            device_id=who, device_id_type=MESH,
        )

    def ring(s):
        return lax.rem(z + s + RING, RING)

    def spot(core, zz, xx):
        return ((core * RING + zz) * 2 + xx) * 2

    base = spot(c, z, x)
    mine = [
        pltpu.make_async_copy(r.at[:, pl.ds(pl.multiple_of(head * D, D), D)], b.at[base + u], local.at[i])
        for i, (r, b) in enumerate(((k_ref, kbuf), (v_ref, vbuf)))
    ]
    for copy in mine:
        copy.start()
    other = pl.ds(pl.multiple_of((1 - head) * D, D), D)
    k_swap = move(k_ref.at[:, other], kbuf.at[base + u], kbuf.at[base + 1 - u], mate)
    v_swap = move(v_ref.at[:, other], vbuf.at[base + u], vbuf.at[base + 1 - u], mate)
    for copy in mine:
        copy.wait()

    late = []

    def blocks(buf, at, count):
        return buf.at[pl.ds(at, count)]

    def same(buf, at, count, who, landed):
        return move(blocks(buf, at, count), blocks(buf, at, count), blocks(buf, landed, count), who)

    def to_sibling(buf, core_spot, count):
        landed = core_spot + (1 - 2 * c) * (POOL // 2)
        late.append(same(buf, core_spot, count, sibling, landed))

    k_swap.wait_recv()
    k_cross = same(kbuf, base, 2, across, spot(c, z, 1 - x))
    v_swap.wait_recv()
    v_up = same(vbuf, base, 2, up, spot(c, ring(-1), x))
    v_down = same(vbuf, base, 2, down, spot(c, ring(1), x))
    v_cross = [same(vbuf, base, 2, across, spot(c, z, 1 - x))]
    crossed = [spot(c, z, 1 - x)]
    to_sibling(vbuf, base, 2)
    k_cross.wait_recv()
    k_up = same(kbuf, spot(c, z, 0), 4, up, spot(c, ring(-1), 0))
    k_down = same(kbuf, spot(c, z, 0), 4, down, spot(c, ring(1), 0))
    to_sibling(kbuf, spot(c, z, 0), 4)

    def forward_v(zz):
        v_cross.append(same(vbuf, spot(c, zz, x), 2, across, spot(c, zz, 1 - x)))
        crossed.append(spot(c, zz, 1 - x))
        to_sibling(vbuf, spot(c, zz, x), 2)

    for s in (1, 2, 3):
        lo, hi = ring(-s), ring(s)
        v_up.wait_recv()
        if s < 3:
            v_up = same(vbuf, spot(c, lo, x), 2, up, spot(c, ring(-s - 1), x))
        else:
            v_up = same(vbuf, spot(c, lo, x), 1, up, spot(c, ring(4), x))
        forward_v(lo)
        v_down.wait_recv()
        if s < 3:
            v_down = same(vbuf, spot(c, hi, x), 2, down, spot(c, ring(s + 1), x))
        else:
            v_down = same(vbuf, spot(c, hi, x) + 1, 1, down, spot(c, ring(4), x) + 1)
        forward_v(hi)
        k_up.wait_recv()
        if s < 3:
            k_up = same(kbuf, spot(c, lo, 0), 4, up, spot(c, ring(-s - 1), 0))
        else:
            k_up = same(kbuf, spot(c, lo, 0), 2, up, spot(c, ring(4), 0))
        to_sibling(kbuf, spot(c, lo, 0), 4)
        k_down.wait_recv()
        if s < 3:
            k_down = same(kbuf, spot(c, hi, 0), 4, down, spot(c, ring(s + 1), 0))
        else:
            k_down = same(kbuf, spot(c, hi, 1), 2, down, spot(c, ring(4), 1))
        to_sibling(kbuf, spot(c, hi, 0), 4)
        done = 1 if s == 1 else 2
        for _ in range(done):
            v_cross.pop(0).wait_recv()
            to_sibling(vbuf, crossed.pop(0), 2)
    far = ring(4)
    v_up.wait_recv()
    v_down.wait_recv()
    forward_v(far)
    k_up.wait_recv()
    k_down.wait_recv()
    to_sibling(kbuf, spot(c, far, 0), 4)
    while v_cross:
        v_cross.pop(0).wait_recv()
        to_sibling(vbuf, crossed.pop(0), 2)
    for copy in late:
        copy.wait_recv()
    for copy in started:
        copy.wait_send()


COPIES = 64


def gathered(keys, values):
    shape = jax.ShapeDtypeStruct((POOL, D, D), BF16)
    vmem = pl.BlockSpec(memory_space=pltpu.VMEM)
    return pl.pallas_call(
        gather_kernel,
        out_shape=(shape, shape),
        in_specs=[vmem, vmem],
        out_specs=(vmem, vmem),
        scratch_shapes=[
            pltpu.SemaphoreType.DMA((COPIES,)),
            pltpu.SemaphoreType.DMA((COPIES,)),
            pltpu.SemaphoreType.DMA((2,)),
        ],
        compiler_params=pltpu.CompilerParams(collective_id=0, has_side_effects=True),
        name="gather_blocks",
    )(keys, values)


def attend_kernel(nw, lst, ga, q_ref, k_ref, v_ref, o_ref, st_ref, qs, bias, acc, mb, lb):
    row = lax.broadcasted_iota(I32, (D, D), 0)
    col = lax.broadcasted_iota(I32, (D, D), 1)
    bias[0] = jnp.zeros((D, D), F32)
    bias[1] = jnp.where(row <= col, 0.0, LOW)
    bias[2] = jnp.full((D, D), LOW, F32)
    for s in range(4):
        for i in range(GROUP):
            qs[s, i * D:(i + 1) * D, :] = q_ref[s * D:(s + 1) * D, i * D:(i + 1) * D]
    for p in range(2):
        acc[0] = jnp.zeros((D, LANES), F32)
        mb[0] = jnp.full((8, LANES), LOW, F32)
        lb[0] = jnp.zeros((8, LANES), F32)
        first_groups = ga[p]

        def step(g, _):
            e0, e1 = lst[p, 2 * g], lst[p, 2 * g + 1]
            owner = (g >= first_groups).astype(I32)
            first = jnp.logical_or(g == 0, g == first_groups)
            i0, i1 = e0 & (POOL - 1), e1 & (POOL - 1)
            k = jnp.concatenate([k_ref[i0], k_ref[i1]], axis=0)
            v = jnp.concatenate([v_ref[i0], v_ref[i1]], axis=0)
            b = jnp.concatenate([bias[e0 >> 6], bias[e1 >> 6]], axis=0)
            vt = v.T
            for w in range(0, LANES, nw):
                q = qs[2 * p + owner, w:w + nw, :]
                s = lax.dot_general(k, q, (((1,), (1,)), ((), ())), preferred_element_type=F32)
                s = s + jnp.concatenate([b] * (nw // D), axis=1)
                old = jnp.where(first, -3e38, mb[g, 0:1, w:w + nw])
                m = jnp.maximum(old, jnp.max(s, axis=0, keepdims=True))
                alpha = jnp.exp2((old - m) * SCALE)
                weights = jnp.exp2((s - m) * SCALE)
                l = lb[g, 0:1, w:w + nw] * alpha + jnp.sum(weights, axis=0, keepdims=True)
                pv = lax.dot_general(
                    vt, weights.astype(BF16), (((1,), (0,)), ((), ())), preferred_element_type=F32
                )
                acc[g + 1, :, w:w + nw] = acc[g, :, w:w + nw] * alpha + pv
                mb[g + 1, 0:1, w:w + nw] = m
                lb[g + 1, 0:1, w:w + nw] = l
            return 0

        lax.fori_loop(0, NG, step, 0)
        for j in range(2):
            at = first_groups if j == 0 else NG
            o_ref[2 * p + j] = acc[at].astype(BF16)
            st_ref[2 * p + j, 0:1] = mb[at, 0:1]
            st_ref[2 * p + j, 1:2] = lb[at, 0:1]


def attended_parts(listing, first_groups, q, k, v):
    vmem = pl.BlockSpec(memory_space=pltpu.VMEM)
    smem = pl.BlockSpec(memory_space=pltpu.SMEM)
    return pl.pallas_call(
        functools.partial(attend_kernel, 128),
        out_shape=(
            jax.ShapeDtypeStruct((4, D, LANES), BF16),
            jax.ShapeDtypeStruct((4, 8, LANES), F32),
        ),
        in_specs=[smem, smem, vmem, vmem, vmem],
        out_specs=(vmem, vmem),
        scratch_shapes=[
            pltpu.VMEM((4, LANES, D), BF16),
            pltpu.VMEM((3, D, D), F32),
            pltpu.VMEM((NG + 1, D, LANES), F32),
            pltpu.VMEM((NG + 1, 8, LANES), F32),
            pltpu.VMEM((NG + 1, 8, LANES), F32),
        ],
        compiler_params=pltpu.CompilerParams(vmem_limit_bytes=VMEM_LIMIT),
        name="attend",
    )(listing, first_groups, q, k, v)


def merge_kernel(o_ref, st_ref, out_ref, ro, rs, send, recv, local):
    ka = lax.axis_index("ka")
    y, c = lax.div(ka, 2), lax.rem(ka, 2)
    barrier = pltpu.get_barrier_semaphore()
    for d in range(1, 8):
        pl.semaphore_signal(barrier, inc=1, device_id={"ka": lax.rem(ka + d, 8)}, device_id_type=MESH)
    pl.semaphore_wait(barrier, 7)

    def remote(src, dst, n, m, who):
        return pltpu.make_async_remote_copy(
            src_ref=src, dst_ref=dst, send_sem=send.at[n], recv_sem=recv.at[m],
            device_id=who, device_id_type=MESH,
        )

    parts = []
    for i in range(4):
        target = (2 * c + i // 2) * 2 + i % 2
        here = target == ka
        away = jnp.logical_not(here)
        for kind, (src, dst) in enumerate(((o_ref, ro), (st_ref, rs))):
            far = remote(src.at[i], dst.at[y], 2 * i + kind, 2 * y + kind, {"ka": target})
            near = pltpu.make_async_copy(src.at[i], dst.at[y], local.at[kind])
            pl.when(away)(far.start)
            pl.when(here)(near.start)
            parts.append((here, away, far, near))
    for yy in range(4):
        own = jnp.logical_and(yy == y, c == lax.div(y, 2))
        for kind, (src, dst) in enumerate(((o_ref, ro), (st_ref, rs))):
            come = remote(src.at[0], dst.at[yy], kind, 2 * yy + kind, {"ka": lax.rem(ka + 1, 8)})
            pl.when(jnp.logical_not(own))(come.wait_recv)
    for here, away, far, near in parts:
        pl.when(here)(near.wait)
    for head, (a, b) in enumerate(((0, 3), (1, 2))):
        ma, mb = rs[a, 0:1], rs[b, 0:1]
        top = jnp.maximum(ma, mb)
        fa, fb = jnp.exp2((ma - top) * SCALE), jnp.exp2((mb - top) * SCALE)
        whole = fa * rs[a, 1:2] + fb * rs[b, 1:2]
        fa, fb = fa / whole, fb / whole
        for i in range(GROUP):
            cut = slice(i * D, (i + 1) * D)
            both = ro[a, :, cut].astype(F32) * fa[:, cut] + ro[b, :, cut].astype(F32) * fb[:, cut]
            at = head * LANES + i * D
            out_ref[:, at:at + D] = both.T.astype(BF16)
    for here, away, far, near in parts:
        pl.when(away)(far.wait_send)


def merged(o, st):
    vmem = pl.BlockSpec(memory_space=pltpu.VMEM)
    return pl.pallas_call(
        merge_kernel,
        out_shape=jax.ShapeDtypeStruct((D, 2 * LANES), BF16),
        in_specs=[vmem, vmem],
        out_specs=vmem,
        scratch_shapes=[
            pltpu.VMEM((4, D, LANES), BF16),
            pltpu.VMEM((4, 8, LANES), F32),
            pltpu.SemaphoreType.DMA((8,)),
            pltpu.SemaphoreType.DMA((8,)),
            pltpu.SemaphoreType.DMA((2,)),
        ],
        compiler_params=pltpu.CompilerParams(collective_id=1, has_side_effects=True),
        name="merge_parts",
    )(o, st)


def in_pool_order(x):
    x = x.reshape(*x.shape[:-1], 2, RING, 2, 2, 2)
    return x


def listing_of(q_order, block_mask, group, core):
    mask = lax.dynamic_slice_in_dim(block_mask, 4 * core, 4, 0).reshape(4, 2, RING, 2, 2, 2)
    order = lax.dynamic_slice_in_dim(q_order, 4 * core, 4, 0)
    mask = lax.dynamic_index_in_dim(mask, group, 3, keepdims=False)
    ids = jnp.arange(2 * POOL, dtype=I32).reshape(2, RING, 2, 2, 2)
    ids = lax.dynamic_index_in_dim(ids, group, 2, keepdims=False)
    mask = mask.transpose(0, 4, 2, 1, 3).reshape(2, 2, POOL)
    ids = ids.transpose(3, 1, 0, 2).reshape(POOL)
    diagonal = (ids[None, None, :] == order.reshape(2, 2, 1)).astype(I32)
    value = jnp.arange(POOL, dtype=I32) + POOL * diagonal
    upto = (jnp.arange(POOL)[:, None] <= jnp.arange(POOL)[None, :]).astype(F32)
    rank = jnp.einsum("pjb,bc->pjc", mask.astype(F32), upto).astype(I32)
    total = rank[:, 0, -1]
    first_groups = jnp.maximum((total + 1) // 2, 1)
    start = jnp.stack([jnp.zeros_like(first_groups), 2 * first_groups], axis=1)
    at = rank - 1 + start[:, :, None]
    hit = (mask[..., None] == 1) & (at[..., None] == jnp.arange(2 * NG, dtype=I32))
    listing = 2 * POOL + jnp.sum(jnp.where(hit, value[..., None] - 2 * POOL, 0), axis=(1, 2))
    return listing.astype(I32), first_groups.astype(I32)


def on_device(queries, keys, values, q_order, block_mask):
    ka = lax.axis_index("ka")
    y, c = ka // 2, ka % 2
    listing, first_groups = listing_of(q_order, block_mask, y // 2, c)
    k, v = gathered(keys.reshape(D, 2 * D), values.reshape(D, 2 * D))
    q = lax.dynamic_slice(queries, (4 * D * c, LANES * head_of(y)), (4 * D, LANES))
    o, st = attended_parts(listing, first_groups, q, k, v)
    return merged(o, st)


def solution(mesh):
    in_specs = (P("pb", "ha"), P("pb", "ka", None, "ha"), P("pb", "ka", None, "ha"), P("pb"), P("pb", None))
    return jax.shard_map(
        on_device, mesh=mesh, in_specs=in_specs, out_specs=P(("pb", "ka"), "ha"), check_vma=False
    )
```

time: 392 us -> 99.6 us (0.25)
  local copies, waits for them, and re-layouts: 127 us -> 6.69 us
  Pallas kernels: 0 us -> 89.7 us
  matrix products: 86.3 us -> 0.13 us
  waiting for transfers between devices: 85.2 us -> 0 us
  other arithmetic: 56.2 us -> 2.73 us
  between operations: 13.2 us -> 0.06 us
  blocking collectives: 10.3 us -> 0 us
  starting transfers between devices: 10 us -> 0 us
    pallas_call x0 -> x3, Pallas kernels: none -> 89.7 us  [the longest x1 37.6 us: gathered(): pl.pallas_call(gather_kernel, out_shape=(shape, shape), in_specs=[vmem, v...]
    dot_general x20 -> x1, matrix products: 86.3 us -> 0.13 us  [listing_of(): rank = jnp.einsum('pjb,bc->pjc', mask.astype(F32), upto).astype(I32)]
    reduce_scatter x1 -> x0, waiting for transfers between devices: 54 us -> none  [sent_together(): lax.psum_scatter(both, axis, scatter_dimension=dim, tiled=True)]
    gather x32 -> x0, local copies, waits for them, and re-layouts: 50.9 us -> none  [the longest x8 24.3 us: unit_scores(): query_rows = jnp.take(query_unit, owners, axis=0)]
    select_n x32 -> x0, other arithmetic: 43.2 us -> none  [the longest x8 36.8 us: unit_scores(): query_rows = jnp.take(query_unit, owners, axis=0)]
    transpose x6 -> x1, local copies, waits for them, and re-layouts: 38.7 us -> 0.1 us  [listing_of(): ids = ids.transpose(3, 1, 0, 2).reshape(POOL)]
    all_gather x2 -> x0, waiting for transfers between devices: 25.4 us -> none  [gather_in_order(): pieces = lax.all_gather(pieces, axes[k])]
    squeeze x20 -> x0, local copies, waits for them, and re-layouts: 11.4 us -> none  [the longest x16 11.4 us: on_device(): row_tops = lax.map(functools.partial(unit_peak, key_pool), unit_args)]
  transfers between devices with their start and end apart: 4 -> 0, of which waited for: 3 -> 0; matrix products, arithmetic and copies ran while one was open for 20% -> 0% of each run, Pallas kernels for 0% -> 0%
where the time goes in v1:
time: 99.6 us; the launch traced here: 99.3 us
  Pallas kernels  89.7 us (90%)
  local copies, waits for them, and re-layouts  6.69 us (7%)
  other arithmetic  2.73 us (3%)
    pallas_call x1, Pallas kernels, gathered(): pl.pallas_call(gather_kernel, out_shape=(shape, shape), in_specs=[vmem, v...  37.6 us
    pallas_call x1, Pallas kernels, attended_parts(): pl.pallas_call(functools.partial(attend_kernel, 128), out_shape=(jax.Shap...  32.6 us
    pallas_call x1, Pallas kernels, merged(): pl.pallas_call(merge_kernel, out_shape=jax.ShapeDtypeStruct((D, 2 * LANES...  19.6 us
    dynamic_slice x1, local copies, waits for them, and re-layouts, on_device(): lax.dynamic_slice(queries, (4 * D * c, LANES * head_of(y)), (4 * D, LANES))  2.31 us

profile of v1, /device:TPU:1, one launch (start us, length us, event | category | flops | bytes accessed | tf_op | source)
XLA Modules:
  0.0 99.3 jit_solution(2831978614924007239)
XLA Ops:
  0.0 0.0 copy-start
  0.0 0.7 dynamic_slice.20
  0.7 0.1 eq.66
  0.8 0.0 copy-done
  0.8 0.1 copy.17
  1.0 0.1 eq.64
  1.1 0.1 copy.13
  1.2 0.6 copy.14
  1.8 0.1 eq.60
  2.0 0.3 copy.15
  2.3 0.1 convert_element_type.20
  2.4 0.1 convolution_convert_fusion
  2.6 0.2 fusion.9
  2.8 0.6 fusion.10.ga
  3.3 0.1 copy.18
  3.4 0.1 stack.4.clone
  3.5 0.1 fusion.8
  3.6 1.3 %fusion = s32[2,34]{1,0:T(2,128)S(1)} fusion(pred[2,2,64]{2,1,0:T(4,128)(4,1)S(1)} %eq.60, s32[2,2,64]{2,1,0:T(2,128)S(1)} %get-tuple-element.13, s32[2,2,64]{2,1,0:T(2,128)S(1)} %get-tuple-element.14), kind=kLoop, calls=%fused_computation.2 | loop fusion | flops 34748 | bytes 2576 | tf_op jit(solution)/shard_map/reduce_sum | solution.py:341
  4.9 0.5 broadcast_add_fusion.lst
  5.4 2.3 %dynamic_slice.21.q_ref = bf16[512,1024]{1,0:T(8,128)(2,1)} dynamic-slice(bf16[1024,2048]{1,0:T(8,128)(2,1)} %param.5, s32[]{:T(128)S(6)} %select_n.56, s32[]{:T(128)S(6)} %select_n.57), dynamic_slice_sizes={512,1024} | dynamic-slice | bytes 2097156 | tf_op jit(solution)/shard_map/dynamic_slice | solution.py:350
  7.7 37.6 %gather_blocks.1 = (bf16[64,128,128]{2,1,0:T(8,128)(2,1)}, bf16[64,128,128]{2,1,0:T(8,128)(2,1)}) custom-call(bf16[128,256]{1,0:T(8,128)(2,1)} %bitcast.31, bf16[128,256]{1,0:T(8,128)(2,1)} %bitcast.32), custom_call_target="tpu_custom_call" | custom-call | tf_op jit(solution)/shard_map/gather_blocks/pallas_call | solution.py:166
  45.3 32.6 %attend.1 = (bf16[4,128,1024]{2,1,0:T(8,128)(2,1)}, f32[4,8,1024]{2,1,0:T(8,128)}) custom-call(s32[2,34]{1,0:T(2,128)} %broadcast_add_fusion.lst, s32[2]{0:T(128)} %fusion.10.ga, bf16[512,1024]{1,0:T(8,128)(2,1)} %dynamic_slice.21.q_ref, bf16[64,128,128]{2,1,0:T(8,128)(2,1)} %get-tuple-element.9.k_ref, bf16[64,128,128]{2,1,0:T(8,128)(2,1)} %get-tuple-element.10.v_ref), custom_call_target="tpu_custom_call" | custom-call | tf_op jit(solution)/shard_map/attend/pallas_call | solution.py:233
  77.9 19.6 %merge_parts.1 = bf16[128,2048]{1,0:T(8,128)(2,1)} custom-call(bf16[4,128,1024]{2,1,0:T(8,128)(2,1)} %get-tuple-element.11.o_ref, f32[4,8,1024]{2,1,0:T(8,128)} %get-tuple-element.12.st_ref), custom_call_target="tpu_custom_call" | custom-call | tf_op jit(solution)/shard_map/merge_parts/pallas_call | solution.py:302
  97.4 1.9 %copy.20 = bf16[128,2048]{1,0:T(8,128)(2,1)} copy(bf16[128,2048]{1,0:T(8,128)(2,1)} %merge_parts.1) | data formatting | bytes 1048576
  (5 shorter events, 0.1 us)
Async XLA Ops:
  0.0 0.8 copy-start
